TPU v7x, 256 devices: a whole 4x4x8 slice. The times are simulated.
256 devices in a mesh: section: 16 (over x_lo, y, core), dp: 16 (over x_hi, z).
Axes of the slice: x: 4 (x_hi: 2, x_lo: 2; x = x_hi * 2 + x_lo), y: 4, z: 8, core: 2. Of those that a mesh axis runs over, the one named last changes fastest.
Arguments:
- inputs: bfloat16 [32768, 8192], P(('section', 'dp')), may hold values from -6 to 6
- hidden_grad: bfloat16 [32768, 1024], P(('section', 'dp')), may hold values from -12 to 12
- gate_pre: bfloat16 [32768, 1024], P(('section', 'dp')), may hold values from -8 to 8
- up_weight: bfloat16 [131072, 1024], P(('section', 'dp')), may hold values from -0.1875 to 0.1875
- row_state: float32 [131072], P(('section', 'dp')), may hold values from 100 to 3000
- col_state: float32 [16384], P('section'), may hold values from 100 to 3000
Outputs:
- upstream: bfloat16 [32768, 8192], P(('section', 'dp'))
- param_step: bfloat16 [131072, 1024], P(('section', 'dp'))
- row_out: float32 [131072], P(('section', 'dp'))
- col_out: float32 [16384], P('section')
All inputs are finite; a program needn't handle non-finite values.
Results may differ from a plain program's by a relative error of at most 0.0049.
Values may be sent and summed in bfloat16 or wider, within the bound.
A program may use at most 128 MiB of HBM per device.

v0:
```python
import jax
import jax.numpy as jnp
from jax import lax
from jax.sharding import PartitionSpec as P

D = 8192
FF = 1024


BETA_TWO = 0.75
TINY_ADD = 1e-30


def shifted(value, axis, steps):
    count = lax.axis_size(axis)
    initial, last = (max(0, -steps), min(count, count - steps))
    return lax.ppermute(value, axis, [(source, source + steps) for source in range(initial, last)])


def local(inputs, hidden_grad, gate_pre, up_weight, row_state, col_state):
    cotangent = (
        hidden_grad.astype(jnp.float32) * jax.nn.silu(gate_pre.astype(jnp.float32))
    ).astype(jnp.bfloat16)
    gathered = lax.all_gather(cotangent, "dp", axis=0, tiled=True)
    columns = lax.all_to_all(inputs, "dp", split_axis=1, concat_axis=0, tiled=True)
    local_block = lax.dot_general(
        gathered, up_weight, (((1,), (1,)), ((), ())), preferred_element_type=jnp.float32
    ).astype(jnp.bfloat16)
    lowered = lax.all_to_all(local_block, "dp", split_axis=0, concat_axis=1, tiled=True)
    gradient = lax.dot_general(
        columns, gathered, (((0,), (0,)), ((), ())), preferred_element_type=jnp.float32
    )
    upstream = shifted(lowered, "section", -1)
    squares = gradient * gradient + TINY_ADD
    row_new = BETA_TWO * row_state + (1.0 - BETA_TWO) * jnp.mean(squares, axis=1)
    entries = float(D) * float(FF)
    col_partial, row_total = lax.psum((jnp.sum(squares, axis=0), jnp.sum(row_new)), "dp")
    col_new = BETA_TWO * col_state + (1.0 - BETA_TWO) * (col_partial / D)
    row_average = row_total / D
    second = row_new[:, None] * col_new[None, :] / row_average
    update = gradient / jnp.sqrt(second)
    grand_total = lax.psum(jnp.sum(update * update), "dp")
    root_mean = jnp.sqrt(grand_total / entries)
    step_out = (update / jnp.maximum(1.0, root_mean)).astype(jnp.bfloat16)
    return (upstream, step_out, row_new, col_new)


def solution(mesh):
    placed = (
        P(("section", "dp"), None),
        P(("section", "dp"), None),
        P(("section", "dp"), None),
        P(("section", "dp"), None),
        P(("section", "dp")),
        P("section"),
    )
    return jax.shard_map(
        local,
        mesh=mesh,
        in_specs=placed,
        out_specs=(
            P(("section", "dp"), None),
            P(("section", "dp"), None),
            P(("section", "dp")),
            P("section"),
        ),
        check_vma=False,
    )
```

profile of v0, /device:TPU:2, one launch (start us, length us, event | category | flops | bytes accessed | tf_op | source)
XLA Modules:
  0.0 330.2 jit_solution(4936819788527266454)
XLA Ops:
  7.2 0.0 copy-start
  7.2 0.0 all-gather.2.cloned.1.call-start
  7.2 2.0 fusion.7
  9.2 0.0 all-gather.2.cloned.1.call-update
  9.2 104.0 %all-gather.2.cloned.1.call-done = bf16[2048,1024]{1,0:T(8,128)(2,1)} async-done(((bf16[128,1024]{1,0:T(8,128)(2,1)}), bf16[2048,1024]{1,0:T(8,128)(2,1)}) %all-gather.2.cloned.1.call-update) | async-done | bytes 4194320 | tf_op jit(solution)/shard_map/all_gather | solution.py:24
  113.3 0.0 copy-done
  113.3 5.9 %convolution_convert_fusion = bf16[2048,512]{1,0:T(8,128)(2,1)} fusion(bf16[2048,1024]{1,0:T(8,128)(2,1)} %all-gather.2.cloned.1.call-done, bf16[512,1024]{1,0:T(8,128)(2,1)S(1)} %copy-done), kind=kOutput, calls=%fused_computation | convolution fusion | flops 2148532224 | bytes 7340032 | tf_op jit(solution)/shard_map/dot_general | solution.py:26
  119.2 5.1 %all-to-all-start = ((bf16[16,128,512]{2,1,0:T(8,128)(2,1)}), bf16[16,128,512]{2,1,0:T(8,128)(2,1)S(1)}, u32[]{:S(2)}, u32[]{:S(2)}) async-start(bf16[16,128,512]{2,1,0:T(8,128)(2,1)} %bitcast.26), calls=%async_computation | async-start | bytes 4194304 | tf_op jit(solution)/shard_map/all_to_all | solution.py:29
  124.2 4.1 %copy.15 = bf16[128,8192]{0,1:T(8,128)(2,1)} copy(bf16[128,8192]{1,0:T(8,128)(2,1)} %param.6) | data formatting | bytes 4194304 | tf_op args[0]
  128.3 43.8 %all-to-all-done = bf16[16,128,512]{2,1,0:T(8,128)(2,1)S(1)} async-done(((bf16[16,128,512]{2,1,0:T(8,128)(2,1)}), bf16[16,128,512]{2,1,0:T(8,128)(2,1)S(1)}, u32[]{:S(2)}, u32[]{:S(2)}) %all-to-all-start) | async-done | bytes 2097184 | tf_op jit(solution)/shard_map/all_to_all | solution.py:29
  172.1 4.5 %all-to-all-start.1 = ((bf16[128,16,512]{0,2,1:T(8,128)(2,1)}), bf16[128,16,512]{0,2,1:T(8,128)(2,1)}, u32[]{:S(2)}, u32[]{:S(2)}) async-start(bf16[128,16,512]{0,2,1:T(8,128)(2,1)} %bitcast.25), calls=%async_computation.1 | async-start | bytes 4194304 | tf_op jit(solution)/shard_map/all_to_all | solution.py:25
  176.7 1.5 copy.18
  178.2 2.9 collective-permute-start
  181.1 45.8 %all-to-all-done.1 = bf16[128,16,512]{0,2,1:T(8,128)(2,1)} async-done(((bf16[128,16,512]{0,2,1:T(8,128)(2,1)}), bf16[128,16,512]{0,2,1:T(8,128)(2,1)}, u32[]{:S(2)}, u32[]{:S(2)}) %all-to-all-start.1) | async-done | bytes 2097184 | tf_op jit(solution)/shard_map/all_to_all | solution.py:25
  226.9 3.9 %copy.16 = bf16[16,128,512]{2,1,0:T(8,128)(2,1)} copy(bf16[16,128,512]{1,2,0:T(8,128)(2,1)} %bitcast.3) | data formatting | bytes 4194304 | tf_op jit(solution)/shard_map/all_to_all | solution.py:25
  230.8 0.0 copy-start.4
  230.8 0.0 copy-start.3
  230.8 5.3 %fusion.1 = (f32[1024]{0:T(1024)S(1)}, f32[512]{0:T(512)S(1)}, f32[1024,512]{1,0:T(8,128)S(1)}) fusion(bf16[2048,1024]{1,0:T(8,128)(2,1)} %all-gather.2.cloned.1.call-done, bf16[2048,512]{1,0:T(8,128)(2,1)} %bitcast.27), kind=kOutput, calls=%fused_computation.6 | convolution fusion | flops 2149579264 | bytes 8394752 | tf_op jit(solution)/shard_map/dot_general | solution.py:30
  236.1 0.0 copy-done.4
  236.2 0.6 fusion.8
  236.8 0.0 copy-start.2
  236.8 39.1 %all-reduce = (f32[]{:T(128)}, f32[1024]{0:T(1024)S(1)}) all-reduce(f32[]{:T(128)} %get-tuple-element.20, f32[1024]{0:T(1024)S(1)} %get-tuple-element.16), channel_id=1, replica_groups=mesh['section'=16,'dp'=16] {'dp'}, use_global_device_ids=true, to_apply=%region_4.5 | all-reduce | flops 1025 | bytes 8200 | tf_op jit(solution)/shard_map/psum | solution.py:37
  276.5 0.0 copy-done.3
  276.6 0.0 copy-start.1
  276.6 1.4 multiply_reduce_fusion
  278.0 37.9 %psum.23 = f32[]{:T(128)} all-reduce(f32[]{:T(128)} %multiply_reduce_fusion), channel_id=1, replica_groups=mesh['section'=16,'dp'=16] {'dp'}, use_global_device_ids=true, to_apply=%region_6.7 | all-reduce | flops 1 | bytes 8 | tf_op jit(solution)/shard_map/psum | solution.py:42
  316.6 1.4 divide_convert_fusion
  318.0 0.0 copy-done.2
  318.0 0.0 copy-done.1
  318.0 2.3 copy.17
  320.3 0.0 collective-permute-done
  320.3 3.1 copy.20
  (1 shorter events, 0.0 us)
Async XLA Ops:
  7.2 106.1 %copy-start = (bf16[512,1024]{1,0:T(8,128)(2,1)S(1)}, bf16[512,1024]{1,0:T(8,128)(2,1)}, u32[]{:S(2)}) copy-start(bf16[512,1024]{1,0:T(8,128)(2,1)} %param.9) | copy-start | bytes 3145732
  7.2 106.1 %all-gather.2.cloned.1.call-start = ((), (), s32[]{:S(2)}) async-start(), calls=%async_computation.2 | async-start | bytes 4456448 | tf_op jit(solution)/shard_map/all_gather | solution.py:24
  119.2 53.0 %all-to-all-start = ((bf16[16,128,512]{2,1,0:T(8,128)(2,1)}), bf16[16,128,512]{2,1,0:T(8,128)(2,1)S(1)}, u32[]{:S(2)}, u32[]{:S(2)}) async-start(bf16[16,128,512]{2,1,0:T(8,128)(2,1)} %bitcast.26), calls=%async_computation | async-start | bytes 4194304 | tf_op jit(solution)/shard_map/all_to_all | solution.py:29
  172.1 54.8 %all-to-all-start.1 = ((bf16[128,16,512]{0,2,1:T(8,128)(2,1)}), bf16[128,16,512]{0,2,1:T(8,128)(2,1)}, u32[]{:S(2)}, u32[]{:S(2)}) async-start(bf16[128,16,512]{0,2,1:T(8,128)(2,1)} %bitcast.25), calls=%async_computation.1 | async-start | bytes 4194304 | tf_op jit(solution)/shard_map/all_to_all | solution.py:25
  178.2 142.1 %collective-permute-start = (bf16[128,8192]{1,0:T(8,128)(2,1)}, bf16[128,8192]{1,0:T(8,128)(2,1)}, u32[]{:S(2)}, u32[]{:S(2)}) collective-permute-start(bf16[128,8192]{1,0:T(8,128)(2,1)} %bitcast.7), channel_id=1, source_target_pairs={{16,0},{32,16},{48,32},{64,48},{80,64},{96,80},{112,96},{128,112},... | collective-permute-start | bytes 6291464 | tf_op jit(solution)/shard_map/ppermute | solution.py:17
  230.8 5.3 %copy-start.4 = (f32[512]{0:T(512)S(1)}, f32[512]{0:T(512)}, u32[]{:S(2)}) copy-start(f32[512]{0:T(512)} %param.10) | copy-start | bytes 6148
  230.8 45.7 %copy-start.3 = (f32[1024]{0:T(1024)S(1)}, f32[1024]{0:T(1024)}, u32[]{:S(2)}) copy-start(f32[1024]{0:T(1024)} %param.11) | copy-start | bytes 12292
  236.8 81.3 %copy-start.2 = (f32[512]{0:T(512)}, f32[512]{0:T(512)S(1)}, u32[]{:S(2)}) copy-start(f32[512]{0:T(512)S(1)} %get-tuple-element.29) | copy-start | bytes 6148
  276.6 41.5 %copy-start.1 = (f32[1024]{0:T(1024)}, f32[1024]{0:T(1024)S(1)}, u32[]{:S(2)}) copy-start(f32[1024]{0:T(1024)S(1)} %multiply_add_fusion) | copy-start | bytes 12292
Sparse Core Ops, SparseCore 0:
  11.2 102.0 all-gather.1
where the time goes:
time: 331 us; the launch traced here: 330 us
  waiting for transfers between devices  194 us (59%)
  blocking collectives  77 us (23%)
  between operations  15.4 us (5%)
  local copies, waits for them, and re-layouts  14.9 us (5%)
  starting transfers between devices  12.5 us (4%)
  matrix products  11.2 us (3%)
  other arithmetic  5.48 us (2%)
    all_gather x1, waiting for transfers between devices, local(): gathered = lax.all_gather(cotangent, 'dp', axis=0, tiled=True)  104 us
    all_to_all x1, waiting for transfers between devices, local(): lax.all_to_all(inputs, 'dp', split_axis=1, concat_axis=0, tiled=True)  45.8 us
    all_to_all x1, waiting for transfers between devices, local(): lax.all_to_all(local_block, 'dp', split_axis=0, concat_axis=1, tiled=True)  43.8 us
    psum x1, blocking collectives, local(): lax.psum((jnp.sum(squares, axis=0), jnp.sum(row_new)), 'dp')  39.1 us
    psum x1, blocking collectives, local(): grand_total = lax.psum(jnp.sum(update * update), 'dp')  37.9 us
    unnamed x13, local copies, waits for them, and re-layouts  9.46 us
  transfers between devices with their start and end apart: 4, of which 3 were waited for; matrix products, arithmetic and copies ran while one was open for 6% of the time, Pallas kernels for 0%

commit v1 on v0

v1 whole, which is shorter than its diff:
```python
import functools

import jax
import jax.numpy as jnp
from jax import lax
from jax.experimental import pallas as pl
from jax.experimental.pallas import tpu as pltpu
from jax.sharding import PartitionSpec as P

D = 8192
FF = 1024
TOK = 128
ROWS = 512
NZ = 8
BETA_TWO = 0.75
TINY_ADD = 1e-30
LAST = 15

MESH = pl.DeviceIdType.MESH
BF = jnp.bfloat16
F32 = jnp.float32

NEAR_FIRST = (1, 7, 2, 6, 3, 5, 4)
FAR_FIRST = (4, 3, 5, 2, 6, 1, 7)


def body(
    x_hbm, hg_hbm, gp_hbm, w_hbm, rstate_hbm, cstate_hbm,
    up_out, step_out, row_out, col_out,
    hg, gp, ctg, w2, xr, lo, grad, gsend, grecv, stepb, rcol, rvec, cvec, smine, spair, sall, zbuf,
    lsem, ag_s, ag_r, w_s, w_r, x_s, x_r, l_s, l_r, g_s, g_r, p_s, p_r, s_s, s_r, o_s, z_s,
):
    s = lax.axis_index("section")
    dp = lax.axis_index("dp")
    xh, z = dp // NZ, dp % NZ

    def ring(k):
        return (z + k) % NZ

    def device(section, half, zz):
        return {"section": section, "dp": half * NZ + zz}

    def remote(src, dst, send, recv, target):
        return pltpu.make_async_remote_copy(
            src_ref=src, dst_ref=dst, send_sem=send, recv_sem=recv, device_id=target, device_id_type=MESH
        )

    barrier = pltpu.get_barrier_semaphore()
    for k in range(1, NZ):
        pl.semaphore_signal(barrier, inc=1, device_id=device(s, xh, ring(k)), device_id_type=MESH)
    pl.semaphore_signal(barrier, inc=1, device_id=device(s, 1 - xh, z), device_id_type=MESH)

    @pl.when(s < LAST)
    def _():
        for k in range(NZ):
            pl.semaphore_signal(barrier, inc=1, device_id=device(s + 1, xh, ring(k)), device_id_type=MESH)

    def columns(half, zz):
        return pl.ds(pl.multiple_of((half * NZ + zz) * ROWS, ROWS), ROWS)

    loads = [
        pltpu.make_async_copy(hg_hbm, hg, lsem.at[0]),
        pltpu.make_async_copy(gp_hbm, gp, lsem.at[1]),
        pltpu.make_async_copy(w_hbm, w2.at[0], lsem.at[2]),
        pltpu.make_async_copy(x_hbm.at[:, columns(1 - xh, z)], xr.at[0, z], lsem.at[3]),
        pltpu.make_async_copy(x_hbm.at[:, columns(xh, z)], xr.at[1, z], lsem.at[4]),
        pltpu.make_async_copy(rstate_hbm, rvec, lsem.at[5]),
        pltpu.make_async_copy(cstate_hbm, cvec, lsem.at[6]),
    ]
    for load in loads:
        load.start()
    loads[0].wait()
    loads[1].wait()

    @pl.loop(0, 4)
    def _(i):
        rows = pl.ds(pl.multiple_of(i * 32, 32), 32)
        v = gp[rows, :].astype(F32)
        ctg[z, rows, :] = (hg[rows, :].astype(F32) * (v / (1.0 + jnp.exp(-v)))).astype(BF)

    pl.semaphore_wait(barrier, NZ + NZ * (s > 0).astype(jnp.int32))

    def gather_step(step):
        copies = []
        for way, d in ((0, 1), (1, -1)):
            block = (z + NZ - d * step) % NZ
            if step < 3:
                ref = ctg.at[block]
            else:
                ref = ctg.at[block, pl.ds(way * (TOK // 2), TOK // 2)]
            copies.append(remote(ref, ref, ag_s.at[way, step], ag_r.at[way, step], device(s, xh, (z + NZ + d) % NZ)))
        return copies

    gathers = [gather_step(step) for step in range(4)]
    weights = remote(w_hbm, w2.at[1], w_s, w_r, device(s, 1 - xh, z))

    def inputs_copy(slot, k):
        half = 1 - xh if slot == 0 else xh
        return remote(
            x_hbm.at[:, columns(half, ring(k))], xr.at[slot, z], x_s.at[slot, k], x_r.at[slot, k], device(s, xh, ring(k))
        )

    inputs_copies = [[inputs_copy(slot, k) for k in FAR_FIRST] for slot in range(2)]

    def lowered_copy(slot, k):
        half = xh if slot == 0 else 1 - xh
        return remote(lo.at[slot, k], up_out.at[:, columns(half, z)], l_s.at[slot, k], l_r.at[slot, k], device(s - 1, xh, ring(k)))

    def lowered(slot, k):
        lo[slot, k] = lax.dot_general(
            ctg[ring(k)], w2[slot], (((1,), (1,)), ((), ())), preferred_element_type=F32
        ).astype(BF)

        @pl.when(s > 0)
        def _():
            lowered_copy(slot, k).start()

    for copy in gathers[0]:
        copy.start()
    weights.start()
    for copy in inputs_copies[0]:
        copy.start()

    zbuf[...] = jnp.zeros_like(zbuf)

    @pl.when(s == LAST)
    def _():
        for i in range(NZ):
            pltpu.make_async_copy(zbuf, up_out.at[:, pl.ds(i * 2 * ROWS, 2 * ROWS)], z_s.at[i]).start()

    loads[2].wait()
    lowered(0, 0)
    for step in range(4):
        for copy in gathers[step]:
            copy.wait_recv()
        if step < 3:
            for copy in gathers[step + 1]:
                copy.start()
        if step == 1:
            for copy in inputs_copies[1]:
                copy.start()
        for k in ((step + 1, NZ - 1 - step) if step < 3 else (4,)):
            lowered(0, k)

    weights.wait_recv()
    for k in (0,) + NEAR_FIRST:
        lowered(1, k)

    def gradient(slot, store):
        for part in range(2):
            cols = pl.ds(part * 256, 256)
            xs = xr[slot, :, :, cols].reshape(NZ * TOK, 256)
            ct = ctg[...].reshape(NZ * TOK, FF)
            store(cols, lax.dot_general(xs, ct, (((0,), (0,)), ((), ())), preferred_element_type=F32))

    for copy in inputs_copies[0]:
        copy.wait_recv()
    loads[3].wait()

    def store_send(rows, value):
        gsend[rows, :] = value.astype(BF)

    gradient(0, store_send)
    partial = remote(gsend, grecv, g_s, g_r, device(s, 1 - xh, z))
    partial.start()

    loads[5].wait()
    loads[6].wait()
    for q in range(4):
        rcol[pl.ds(q * 128, 128), :] = jnp.transpose(jnp.broadcast_to(rvec[pl.ds(q, 1), :], (128, 128)))

    for copy in inputs_copies[1]:
        copy.wait_recv()
    loads[4].wait()

    def store_own(rows, value):
        grad[rows, :] = value

    gradient(1, store_own)
    partial.wait_recv()

    def tile(q):
        return pl.ds(pl.multiple_of(q * 128, 128), 128)

    def squares_step(q, rowsum):
        g = grad[:, tile(q)] + grecv[:, tile(q)].astype(F32)
        grad[:, tile(q)] = g
        sq = g * g + TINY_ADD
        smine[pl.ds(q, 1), :] = jnp.sum(sq, axis=0, keepdims=True)
        return rowsum + sq

    rowsum = lax.fori_loop(0, 8, squares_step, jnp.zeros((ROWS, 128), F32))
    rowmean = jnp.sum(rowsum, axis=1, keepdims=True) * (1.0 / FF)
    rnew = BETA_TWO * rcol[...] + (1.0 - BETA_TWO) * jnp.broadcast_to(rowmean, (ROWS, 128))
    rcol[...] = rnew
    rinv = 1.0 / rnew

    def weighted_step(q, carry):
        g = grad[:, tile(q)]
        smine[pl.ds(8 + q, 1), :] = jnp.sum(g * g * rinv, axis=0, keepdims=True)
        return carry

    lax.fori_loop(0, 8, weighted_step, 0)
    smine[pl.ds(16, 8), :] = jnp.broadcast_to(jnp.sum(rnew, axis=0, keepdims=True), (8, 128))

    pair = remote(smine, spair, p_s, p_r, device(s, 1 - xh, z))
    pair.start()
    for q in range(4):
        rvec[pl.ds(q, 1), :] = jnp.transpose(rcol[pl.ds(q * 128, 128), :])[0:1, :]
    row_copy = pltpu.make_async_copy(rvec, row_out, o_s.at[0])
    row_copy.start()
    pair.wait_recv()
    sall[0] = smine[...] + spair[...]
    sums = [remote(sall.at[0], sall.at[k], s_s.at[k], s_r.at[k], device(s, xh, ring(k))) for k in FAR_FIRST]
    for copy in sums:
        copy.start()
    for copy in sums:
        copy.wait_recv()
    total = sall[(NZ - 0 + z) % NZ]
    for i in range(1, NZ):
        total = total + sall[(NZ - i + z) % NZ]
    cnew = BETA_TWO * cvec[...] + (1.0 - BETA_TWO) * (total[0:8] * (1.0 / D))
    cvec[...] = cnew
    col_copy = pltpu.make_async_copy(cvec, col_out, o_s.at[1])
    col_copy.start()
    average = total[16:17, :] * (1.0 / D)
    ratio = jnp.sum(jnp.sum(total[8:16] / cnew, axis=0, keepdims=True), axis=1, keepdims=True)
    root = jnp.sqrt(jnp.broadcast_to(ratio, (1, 128)) * average * (1.0 / (float(D) * float(FF))))
    scale = jnp.sqrt(average) / jnp.maximum(1.0, root)
    rowfac = lax.rsqrt(rcol[...]) * scale
    smine_free = lax.rsqrt(cnew)
    spair[pl.ds(0, 8), :] = smine_free

    def update_step(q, carry):
        stepb[:, tile(q)] = (grad[:, tile(q)] * rowfac * spair[pl.ds(q, 1), :]).astype(BF)
        return carry

    lax.fori_loop(0, 8, update_step, 0)
    step_copy = pltpu.make_async_copy(stepb, step_out, o_s.at[2])
    step_copy.start()

    for copies in gathers:
        for copy in copies:
            copy.wait_send()
    weights.wait_send()
    for copies in inputs_copies:
        for copy in copies:
            copy.wait_send()
    partial.wait_send()
    pair.wait_send()
    for copy in sums:
        copy.wait_send()

    @pl.when(s > 0)
    def _():
        for slot in range(2):
            for k in range(NZ):
                lowered_copy(slot, k).wait_send()

    @pl.when(s < LAST)
    def _():
        for slot in range(2):
            for k in range(NZ):
                lowered_copy(slot, k).wait_recv()

    @pl.when(s == LAST)
    def _():
        for i in range(NZ):
            pltpu.make_async_copy(zbuf, up_out.at[:, pl.ds(i * 2 * ROWS, 2 * ROWS)], z_s.at[i]).wait()

    row_copy.wait()
    col_copy.wait()
    step_copy.wait()


def local(inputs, hidden_grad, gate_pre, up_weight, row_state, col_state):
    hbm = pl.BlockSpec(memory_space=pl.ANY)
    dma = pltpu.SemaphoreType.DMA
    upstream, step_out, row_new, col_new = pl.pallas_call(
        body,
        name="relay_step",
        out_shape=(
            jax.ShapeDtypeStruct((TOK, D), BF),
            jax.ShapeDtypeStruct((ROWS, FF), BF),
            jax.ShapeDtypeStruct((ROWS // 128, 128), F32),
            jax.ShapeDtypeStruct((FF // 128, 128), F32),
        ),
        in_specs=[hbm] * 6,
        out_specs=(hbm,) * 4,
        scratch_shapes=[
            pltpu.VMEM((TOK, FF), BF),
            pltpu.VMEM((TOK, FF), BF),
            pltpu.VMEM((NZ, TOK, FF), BF),
            pltpu.VMEM((2, ROWS, FF), BF),
            pltpu.VMEM((2, NZ, TOK, ROWS), BF),
            pltpu.VMEM((2, NZ, TOK, ROWS), BF),
            pltpu.VMEM((ROWS, FF), F32),
            pltpu.VMEM((ROWS, FF), BF),
            pltpu.VMEM((ROWS, FF), BF),
            pltpu.VMEM((ROWS, FF), BF),
            pltpu.VMEM((ROWS, 128), F32),
            pltpu.VMEM((ROWS // 128, 128), F32),
            pltpu.VMEM((FF // 128, 128), F32),
            pltpu.VMEM((24, 128), F32),
            pltpu.VMEM((24, 128), F32),
            pltpu.VMEM((NZ, 24, 128), F32),
            pltpu.VMEM((TOK, 2 * ROWS), BF),
            dma((7,)),
            dma((2, 4)), dma((2, 4)),
            dma(()), dma(()),
            dma((2, NZ)), dma((2, NZ)),
            dma((2, NZ)), dma((2, NZ)),
            dma(()), dma(()),
            dma(()), dma(()),
            dma((NZ,)), dma((NZ,)),
            dma((3,)),
            dma((NZ,)),
        ],
        compiler_params=pltpu.CompilerParams(collective_id=0, has_side_effects=True, vmem_limit_bytes=32 << 20),
        cost_estimate=pl.CostEstimate(flops=4 * 1024 * 1024 * 1024, transcendentals=TOK * FF, bytes_accessed=8 << 20),
    )(
        inputs, hidden_grad, gate_pre, up_weight,
        row_state.reshape(ROWS // 128, 128), col_state.reshape(FF // 128, 128),
    )
    return upstream, step_out, row_new.reshape(ROWS), col_new.reshape(FF)


def solution(mesh):
    rows = P(("section", "dp"), None)
    placed = (rows, rows, rows, rows, P(("section", "dp")), P("section"))
    return jax.shard_map(
        local,
        mesh=mesh,
        in_specs=placed,
        out_specs=(rows, rows, P(("section", "dp")), P("section")),
        check_vma=False,
    )
```

time: 331 us -> 148 us (0.45)
  waiting for transfers between devices: 194 us -> 0 us
  Pallas kernels: 0 us -> 137 us
  blocking collectives: 77 us -> 0 us
  between operations: 15.4 us -> 0.66 us
  starting transfers between devices: 12.5 us -> 0 us
  matrix products: 11.2 us -> 0 us
  other arithmetic: 5.48 us -> 0 us
  local copies, waits for them, and re-layouts: 14.9 us -> 9.54 us
    pallas_call x0 -> x1, Pallas kernels: none -> 137 us  [local(): pl.pallas_call(body, name='relay_step', out_shape=(jax.ShapeDtypeStruct((...]
    all_gather x1 -> x0, waiting for transfers between devices: 104 us -> none  [local(): gathered = lax.all_gather(cotangent, 'dp', axis=0, tiled=True)]
    all_to_all x2 -> x0, waiting for transfers between devices: 89.6 us -> none  [the longest x1 45.8 us: local(): lax.all_to_all(inputs, 'dp', split_axis=1, concat_axis=0, tiled=True)]
    psum x2 -> x0, blocking collectives: 77 us -> none  [the longest x1 39.1 us: local(): lax.psum((jnp.sum(squares, axis=0), jnp.sum(row_new)), 'dp')]
    dot_general x2 -> x0, matrix products: 11.2 us -> none  [the longest x1 5.89 us: local(): lax.dot_general(gathered, up_weight, (((1,), (1,)), ((), ())), preferred_...]
    all_to_all x2 -> x0, starting transfers between devices: 9.6 us -> none  [the longest x1 5.06 us: local(): lax.all_to_all(local_block, 'dp', split_axis=0, concat_axis=1, tiled=True)]
    all_to_all x2 -> x0, local copies, waits for them, and re-layouts: 5.45 us -> none  [the longest x1 3.91 us: local(): lax.all_to_all(inputs, 'dp', split_axis=1, concat_axis=0, tiled=True)]
    convert_element_type x2 -> x0, other arithmetic: 3.42 us -> none  [the longest x1 1.98 us: local(): cotangent = (hidden_grad.astype(jnp.float32) * jax.nn.silu(gate_pre.astyp...]
  transfers between devices with their start and end apart: 4 -> 0, of which waited for: 3 -> 0; matrix products, arithmetic and copies ran while one was open for 6% -> 0% of each run, Pallas kernels for 0% -> 0%
where the time goes in v1:
time: 148 us; the launch traced here: 147 us
  Pallas kernels  137 us (93%)
  local copies, waits for them, and re-layouts  9.54 us (6%)
    pallas_call x1, Pallas kernels, local(): pl.pallas_call(body, name='relay_step', out_shape=(jax.ShapeDtypeStruct((...  137 us
    unnamed x16, local copies, waits for them, and re-layouts  9.54 us

profile of v1, /device:TPU:2, one launch (start us, length us, event | category | flops | bytes accessed | tf_op | source)
XLA Modules:
  0.0 147.4 jit_solution(3230147142118785379)
XLA Ops:
  0.6 0.0 copy-start
  0.6 1.6 %copy-done = bf16[128,8192]{1,0:T(8,128)(2,1)S(1)} copy-done((bf16[128,8192]{1,0:T(8,128)(2,1)S(1)}, bf16[128,8192]{1,0:T(8,128)(2,1)}, u32[]{:S(2)}) %copy-start) | copy-done | bytes 2097176
  2.2 0.0 copy-start.1
  2.2 1.2 copy-done.1
  3.5 0.0 copy-start.2
  3.5 0.9 copy-done.2
  4.4 0.0 copy-start.3
  4.4 0.9 copy-done.3
  5.4 0.0 copy-start.4
  5.4 0.7 copy-done.4
  6.0 0.0 copy-start.5
  6.0 0.7 copy-done.5
  6.7 137.2 %relay_step.1 = (bf16[128,8192]{1,0:T(8,128)(2,1)S(1)}, bf16[512,1024]{1,0:T(8,128)(2,1)S(1)}, f32[4,128]{1,0:T(4,128)S(1)}, f32[8,128]{1,0:T(8,128)S(1)}) custom-call(bf16[128,8192]{1,0:T(8,128)(2,1)S(1)} %copy-done, bf16[128,1024]{1,0:T(8,128)(2,1)S(1)} %copy-done.2, bf16[128,1024]{1,0:T(8,128)(2,1)S(1)} %copy-done.3, bf16[512,1024]{1,0:T(8,128)(2,1)S(1)} %copy-done.1, ...), custom_call_target="tpu_custom_call" | custom-call | flops 4294967296 | bytes 8388608 | tf_op jit(solution)/shard_map/relay_step/pallas_call | solution.py:279
  143.9 1.3 copy.14
  145.2 1.0 copy.15
  146.2 0.6 copy.16
  146.8 0.6 copy.17
Async XLA Ops:
  0.6 1.6 %copy-start = (bf16[128,8192]{1,0:T(8,128)(2,1)S(1)}, bf16[128,8192]{1,0:T(8,128)(2,1)}, u32[]{:S(2)}) copy-start(bf16[128,8192]{1,0:T(8,128)(2,1)} %x_hbm.1) | copy-start | bytes 6291460
  2.2 1.2 copy-start.1
  3.5 0.9 copy-start.2
  4.4 0.9 copy-start.3
  5.4 0.7 copy-start.4
  6.0 0.7 copy-start.5

commit v2 on v1

--- a/solution.py
+++ b/solution.py
@@ -136,15 +136,11 @@
         if step < 3:
             for copy in gathers[step + 1]:
                 copy.start()
-        if step == 1:
+        if step == 3:
             for copy in inputs_copies[1]:
                 copy.start()
         for k in ((step + 1, NZ - 1 - step) if step < 3 else (4,)):
             lowered(0, k)
-
-    weights.wait_recv()
-    for k in (0,) + NEAR_FIRST:
-        lowered(1, k)
 
     def gradient(slot, store):
         for part in range(2):
@@ -163,6 +159,10 @@
     gradient(0, store_send)
     partial = remote(gsend, grecv, g_s, g_r, device(s, 1 - xh, z))
     partial.start()
+
+    weights.wait_recv()
+    for k in (0,) + NEAR_FIRST:
+        lowered(1, k)
 
     loads[5].wait()
     loads[6].wait()
@@ -271,6 +271,15 @@
     row_copy.wait()
     col_copy.wait()
     step_copy.wait()
+
+
+def place(*refs):
+    ins, outs, sem = refs[:4], refs[4:8], refs[8]
+    copies = [pltpu.make_async_copy(a, b, sem.at[i]) for i, (a, b) in enumerate(zip(ins, outs))]
+    for copy in copies:
+        copy.start()
+    for copy in copies:
+        copy.wait()
 
 
 def local(inputs, hidden_grad, gate_pre, up_weight, row_state, col_state):
@@ -319,9 +328,21 @@
         compiler_params=pltpu.CompilerParams(collective_id=0, has_side_effects=True, vmem_limit_bytes=32 << 20),
         cost_estimate=pl.CostEstimate(flops=4 * 1024 * 1024 * 1024, transcendentals=TOK * FF, bytes_accessed=8 << 20),
     )(
-        inputs, hidden_grad, gate_pre, up_weight,
-        row_state.reshape(ROWS // 128, 128), col_state.reshape(FF // 128, 128),
+        *(
+            pltpu.with_memory_space_constraint(v, pltpu.HBM)
+            for v in (inputs, hidden_grad, gate_pre, up_weight, row_state.reshape(ROWS // 128, 128), col_state.reshape(FF // 128, 128))
+        )
     )
+    results = (upstream, step_out, row_new, col_new)
+    upstream, step_out, row_new, col_new = pl.pallas_call(
+        place,
+        name="place_outputs",
+        out_shape=tuple(jax.ShapeDtypeStruct(v.shape, v.dtype) for v in results),
+        in_specs=[hbm] * 4,
+        out_specs=tuple([pl.BlockSpec(memory_space=pltpu.HBM)] * 4),
+        scratch_shapes=[dma((4,))],
+        compiler_params=pltpu.CompilerParams(vmem_limit_bytes=1 << 20),
+    )(*results)
     return upstream, step_out, row_new.reshape(ROWS), col_new.reshape(FF)
 
 

time: 148 us -> 126 us (0.85)
  Pallas kernels: 137 us -> 125 us
  local copies, waits for them, and re-layouts: 9.54 us -> 0 us
    pallas_call x1, Pallas kernels: 137 us -> 123 us  [local(): pl.pallas_call(body, name='relay_step', out_shape=(jax.ShapeDtypeStruct((...]
    unnamed x16 -> x0, local copies, waits for them, and re-layouts: 9.54 us -> none
    pallas_call x0 -> x1, Pallas kernels: none -> 1.7 us  [local(): pl.pallas_call(place, name='place_outputs', out_shape=tuple((jax.ShapeDty...]
where the time goes in v2:
time: 126 us
  Pallas kernels  125 us (99%)
    pallas_call x1, Pallas kernels, local(): pl.pallas_call(body, name='relay_step', out_shape=(jax.ShapeDtypeStruct((...  123 us

profile of v2, /device:TPU:2, one launch (start us, length us, event | category | flops | bytes accessed | tf_op | source)
XLA Modules:
  0.0 125.7 jit_solution(11362434969440333615)
XLA Ops:
  0.6 123.3 %relay_step.1 = (bf16[128,8192]{1,0:T(8,128)(2,1)S(1)}, bf16[512,1024]{1,0:T(8,128)(2,1)S(1)}, f32[4,128]{1,0:T(4,128)S(1)}, f32[8,128]{1,0:T(8,128)S(1)}) custom-call(bf16[128,8192]{1,0:T(8,128)(2,1)} %x_hbm.1, bf16[128,1024]{1,0:T(8,128)(2,1)} %hg_hbm.1, bf16[128,1024]{1,0:T(8,128)(2,1)} %gp_hbm.1, bf16[512,1024]{1,0:T(8,128)(2,1)} %w_hbm.1, ...), custom_call_target="tpu_custom_call" | custom-call | flops 4294967296 | bytes 8388608 | tf_op jit(solution)/shard_map/relay_step/pallas_call | solution.py:288
  124.0 1.7 %place_outputs.1 = (bf16[128,8192]{1,0:T(8,128)(2,1)}, bf16[512,1024]{1,0:T(8,128)(2,1)}, f32[4,128]{1,0:T(4,128)}, f32[8,128]{1,0:T(8,128)}) custom-call(bf16[128,8192]{1,0:T(8,128)(2,1)S(1)} %get-tuple-element.12.refs_0_, bf16[512,1024]{1,0:T(8,128)(2,1)S(1)} %get-tuple-element.13.refs_1_, f32[4,128]{1,0:T(4,128)S(1)} %get-tuple-element.14.refs_2_, ...), custom_call_target="tpu_custom_call" | custom-call | tf_op jit(solution)/shard_map/place_outputs/pallas_call | solution.py:337

commit v3 on v2

--- a/solution.py
+++ b/solution.py
@@ -16,19 +16,26 @@
 TINY_ADD = 1e-30
 LAST = 15
 
+GROUPS = (
+    ((0, 4),), ((1, 4),), ((0, 3), (0, 1)), ((0, 5), (0, 7)), ((1, 3), (1, 1)), ((1, 5), (1, 7)), ((0, 2), (0, 6)), ((1, 2), (1, 6)),
+)
+GROUP_OF = {pair: i for i, group in enumerate(GROUPS) for pair in group}
+
 MESH = pl.DeviceIdType.MESH
 BF = jnp.bfloat16
 F32 = jnp.float32
 
 NEAR_FIRST = (1, 7, 2, 6, 3, 5, 4)
 FAR_FIRST = (4, 3, 5, 2, 6, 1, 7)
+INPUT_ORDER = (((0, 1), (0, 7), (1, 1), (1, 7)), ((0, 2), (0, 6)), ((0, 3), (0, 5)), ((0, 4), (1, 4), (1, 3), (1, 5), (1, 2), (1, 6)), ())
+ORDER = tuple((slot, k) for slot in range(2) for k in FAR_FIRST)
 
 
 def body(
     x_hbm, hg_hbm, gp_hbm, w_hbm, rstate_hbm, cstate_hbm,
     up_out, step_out, row_out, col_out,
-    hg, gp, ctg, w2, xr, lo, grad, gsend, grecv, stepb, rcol, rvec, cvec, smine, spair, sall, zbuf,
-    lsem, ag_s, ag_r, w_s, w_r, x_s, x_r, l_s, l_r, g_s, g_r, p_s, p_r, s_s, s_r, o_s, z_s,
+    hg, gp, ctg, w2, xr, lo, grad, gsend, grecv, rcol, rvec, cvec, smine, sred, sgat, zbuf, passed,
+    lsem, ag_s, ag_r, w_s, w_r, x_s, x_r, l_s, l_r, g_s, g_r, p_s, p_r, s_s, s_r, z_s, r_r, f_s, ready,
 ):
     s = lax.axis_index("section")
     dp = lax.axis_index("dp")
@@ -46,14 +53,20 @@
         )
 
     barrier = pltpu.get_barrier_semaphore()
-    for k in range(1, NZ):
-        pl.semaphore_signal(barrier, inc=1, device_id=device(s, xh, ring(k)), device_id_type=MESH)
-    pl.semaphore_signal(barrier, inc=1, device_id=device(s, 1 - xh, z), device_id_type=MESH)
+    def greet(sem, target):
+        pl.semaphore_signal(sem, inc=1, device_id=target, device_id_type=MESH)
+
+    for k in (1, NZ - 1):
+        greet(barrier, device(s, xh, ring(k)))
+    greet(barrier, device(s, 1 - xh, z))
 
     @pl.when(s < LAST)
     def _():
-        for k in range(NZ):
-            pl.semaphore_signal(barrier, inc=1, device_id=device(s + 1, xh, ring(k)), device_id_type=MESH)
+        greet(barrier, device(s + 1, xh, z))
+
+    @pl.when(s > 0)
+    def _():
+        greet(barrier, device(s - 1, xh, z))
 
     def columns(half, zz):
         return pl.ds(pl.multiple_of((half * NZ + zz) * ROWS, ROWS), ROWS)
@@ -78,7 +91,7 @@
         v = gp[rows, :].astype(F32)
         ctg[z, rows, :] = (hg[rows, :].astype(F32) * (v / (1.0 + jnp.exp(-v)))).astype(BF)
 
-    pl.semaphore_wait(barrier, NZ + NZ * (s > 0).astype(jnp.int32))
+    pl.semaphore_wait(barrier, 3 + (s > 0).astype(jnp.int32) + (s < LAST).astype(jnp.int32))
 
     def gather_step(step):
         copies = []
@@ -100,26 +113,68 @@
             x_hbm.at[:, columns(half, ring(k))], xr.at[slot, z], x_s.at[slot, k], x_r.at[slot, k], device(s, xh, ring(k))
         )
 
-    inputs_copies = [[inputs_copy(slot, k) for k in FAR_FIRST] for slot in range(2)]
+    inputs_copies = [{k: inputs_copy(slot, k) for k in FAR_FIRST} for slot in range(2)]
 
     def lowered_copy(slot, k):
         half = xh if slot == 0 else 1 - xh
         return remote(lo.at[slot, k], up_out.at[:, columns(half, z)], l_s.at[slot, k], l_r.at[slot, k], device(s - 1, xh, ring(k)))
 
-    def lowered(slot, k):
+    crossing = (s > 0) & (s % 2 == 0)
+
+    def relay_copy(slot, k):
+        return remote(lo.at[slot, k], passed.at[slot, k], l_s.at[slot, k], r_r.at[slot, k], device(s - 1, xh, z))
+
+    def forward_copy(slot, k):
+        half = xh if slot == 0 else 1 - xh
+        return remote(
+            passed.at[slot, k], up_out.at[:, columns(half, z)], f_s.at[slot, k], l_r.at[slot, k], device(s, xh, ring(k))
+        )
+
+    def lowered_send(pairs):
+        for slot, k in pairs:
+            direct = s > 0
+            if k:
+                direct = direct & ~(crossing & (GROUP_OF[slot, k] < NZ - s // 2))
+
+            @pl.when(direct)
+            def _():
+                lowered_copy(slot, k).start()
+
+    def relay_send():
+        for i, group in enumerate(GROUPS):
+
+            @pl.when(crossing & (i < NZ - s // 2))
+            def _():
+                for slot, k in group:
+                    relay_copy(slot, k).start()
+
+    def pass_on(first, last, action):
+        for i in range(first, last):
+
+            @pl.when((s % 2 == 1) & (i < NZ - (s + 1) // 2))
+            def _():
+                for slot, k in GROUPS[i]:
+                    action(slot, k)
+
+    def pass_start(slot, k):
+        relay_copy(slot, k).wait_recv()
+        forward_copy(slot, k).start()
+
+    def lowered(slot, k, send=True):
         lo[slot, k] = lax.dot_general(
             ctg[ring(k)], w2[slot], (((1,), (1,)), ((), ())), preferred_element_type=F32
         ).astype(BF)
-
-        @pl.when(s > 0)
-        def _():
-            lowered_copy(slot, k).start()
+        if send:
+            lowered_send(((slot, k),))
+
+    def send_inputs(step):
+        for slot, k in INPUT_ORDER[step]:
+            inputs_copies[slot][k].start()
 
     for copy in gathers[0]:
         copy.start()
     weights.start()
-    for copy in inputs_copies[0]:
-        copy.start()
+    send_inputs(0)
 
     zbuf[...] = jnp.zeros_like(zbuf)
 
@@ -130,17 +185,26 @@
 
     loads[2].wait()
     lowered(0, 0)
+
     for step in range(4):
         for copy in gathers[step]:
             copy.wait_recv()
         if step < 3:
             for copy in gathers[step + 1]:
                 copy.start()
-        if step == 3:
-            for copy in inputs_copies[1]:
-                copy.start()
+        send_inputs(step + 1)
+        if step == 2:
+
+            @pl.when(s < LAST)
+            def _():
+                greet(ready, device(s + 1, xh, z))
+
         for k in ((step + 1, NZ - 1 - step) if step < 3 else (4,)):
-            lowered(0, k)
+            lowered(0, k, send=False)
+
+    @pl.when(s > 0)
+    def _():
+        pl.semaphore_wait(ready, 1)
 
     def gradient(slot, store):
         for part in range(2):
@@ -149,7 +213,7 @@
             ct = ctg[...].reshape(NZ * TOK, FF)
             store(cols, lax.dot_general(xs, ct, (((0,), (0,)), ((), ())), preferred_element_type=F32))
 
-    for copy in inputs_copies[0]:
+    for copy in inputs_copies[0].values():
         copy.wait_recv()
     loads[3].wait()
 
@@ -161,16 +225,19 @@
     partial.start()
 
     weights.wait_recv()
-    for k in (0,) + NEAR_FIRST:
-        lowered(1, k)
+    for k in range(NZ):
+        lowered(1, k, send=k == 0)
+    relay_send()
+    lowered_send(ORDER[0:4])
 
     loads[5].wait()
     loads[6].wait()
     for q in range(4):
         rcol[pl.ds(q * 128, 128), :] = jnp.transpose(jnp.broadcast_to(rvec[pl.ds(q, 1), :], (128, 128)))
 
-    for copy in inputs_copies[1]:
+    for copy in inputs_copies[1].values():
         copy.wait_recv()
+    lowered_send(ORDER[4:7])
     loads[4].wait()
 
     def store_own(rows, value):
@@ -180,75 +247,94 @@
     partial.wait_recv()
 
     def tile(q):
-        return pl.ds(pl.multiple_of(q * 128, 128), 128)
-
-    def squares_step(q, rowsum):
-        g = grad[:, tile(q)] + grecv[:, tile(q)].astype(F32)
-        grad[:, tile(q)] = g
-        sq = g * g + TINY_ADD
-        smine[pl.ds(q, 1), :] = jnp.sum(sq, axis=0, keepdims=True)
-        return rowsum + sq
-
-    rowsum = lax.fori_loop(0, 8, squares_step, jnp.zeros((ROWS, 128), F32))
-    rowmean = jnp.sum(rowsum, axis=1, keepdims=True) * (1.0 / FF)
-    rnew = BETA_TWO * rcol[...] + (1.0 - BETA_TWO) * jnp.broadcast_to(rowmean, (ROWS, 128))
-    rcol[...] = rnew
-    rinv = 1.0 / rnew
-
-    def weighted_step(q, carry):
-        g = grad[:, tile(q)]
-        smine[pl.ds(8 + q, 1), :] = jnp.sum(g * g * rinv, axis=0, keepdims=True)
-        return carry
-
-    lax.fori_loop(0, 8, weighted_step, 0)
-    smine[pl.ds(16, 8), :] = jnp.broadcast_to(jnp.sum(rnew, axis=0, keepdims=True), (8, 128))
-
-    pair = remote(smine, spair, p_s, p_r, device(s, 1 - xh, z))
-    pair.start()
-    for q in range(4):
-        rvec[pl.ds(q, 1), :] = jnp.transpose(rcol[pl.ds(q * 128, 128), :])[0:1, :]
-    row_copy = pltpu.make_async_copy(rvec, row_out, o_s.at[0])
-    row_copy.start()
-    pair.wait_recv()
-    sall[0] = smine[...] + spair[...]
-    sums = [remote(sall.at[0], sall.at[k], s_s.at[k], s_r.at[k], device(s, xh, ring(k))) for k in FAR_FIRST]
+        return pl.ds(q * 128, 128)
+
+    def fold(v):
+        return (v[0:8] + v[8:16]) + (v[16:24] + v[24:32])
+
+    def stats_step(i, carry):
+        us, vs, rsum = carry
+        rows = pl.ds(pl.multiple_of(i * 32, 32), 32)
+        squares = []
+        for q in range(8):
+            g = grad[rows, tile(q)] + grecv[rows, tile(q)].astype(F32)
+            grad[rows, tile(q)] = g
+            squares.append(g * g)
+        rowsum = ((squares[0] + squares[1]) + (squares[2] + squares[3])) + ((squares[4] + squares[5]) + (squares[6] + squares[7]))
+        rowmean = jnp.sum(rowsum, axis=1, keepdims=True) * (1.0 / FF) + TINY_ADD
+        rnew = BETA_TWO * rcol[rows, :] + (1.0 - BETA_TWO) * jnp.broadcast_to(rowmean, (32, 128))
+        rcol[rows, :] = rnew
+        rinv = 1.0 / rnew
+        us = tuple(u + fold(sq) for u, sq in zip(us, squares))
+        vs = tuple(v + fold(sq * rinv) for v, sq in zip(vs, squares))
+        return us, vs, rsum + fold(rnew)
+
+    zero = jnp.zeros((8, 128), F32)
+    us, vs, rsum = lax.fori_loop(0, ROWS // 32, stats_step, ((zero,) * 8, (zero,) * 8, zero))
+    rsum = jnp.sum(rsum, axis=0, keepdims=True)
+    for q in range(8):
+        smine[q, 0:1] = jnp.sum(us[q], axis=0, keepdims=True) + ROWS * TINY_ADD
+        smine[q, 1:2] = jnp.sum(vs[q], axis=0, keepdims=True)
+        smine[q, 2:3] = rsum
+        smine[q, 3:4] = rsum
+
+    sums = []
+    for other in range(2):
+        half = 1 - xh if other else xh
+        for k in FAR_FIRST + ((0,) if other else ()):
+            sums.append(remote(smine.at[ring(k)], sred.at[xh, z], s_s.at[other, k], s_r.at[other, k], device(s, half, ring(k))))
     for copy in sums:
         copy.start()
+    lowered_send(ORDER[7:10])
+    pass_on(0, 4, pass_start)
+    sred[xh, z] = smine[z]
+    for q in range(4):
+        row_out[pl.ds(q, 1), :] = jnp.transpose(rcol[pl.ds(q * 128, 128), :])[0:1, :]
     for copy in sums:
         copy.wait_recv()
-    total = sall[(NZ - 0 + z) % NZ]
+    total = sred[0, 0]
+    for i in range(1, 2 * NZ):
+        total = total + sred[i // NZ, i % NZ]
+    cnew = BETA_TWO * cvec[pl.ds(z, 1), :] + (1.0 - BETA_TWO) * (total[0:1] * (1.0 / D))
+    sgat[z, 0:1] = cnew
+    sgat[z, 1:2] = total[1:2] / cnew
+    shares = [remote(sgat.at[z], sgat.at[z], p_s.at[k], p_r.at[k], device(s, xh, ring(k))) for k in FAR_FIRST]
+    for copy in shares:
+        copy.start()
+    pass_on(4, NZ, pass_start)
+    lowered_send(ORDER[10:14])
+    average = total[2:3] * (1.0 / D)
+    for copy in shares:
+        copy.wait_recv()
+    ratio = sgat[0, 1:2]
     for i in range(1, NZ):
-        total = total + sall[(NZ - i + z) % NZ]
-    cnew = BETA_TWO * cvec[...] + (1.0 - BETA_TWO) * (total[0:8] * (1.0 / D))
-    cvec[...] = cnew
-    col_copy = pltpu.make_async_copy(cvec, col_out, o_s.at[1])
-    col_copy.start()
-    average = total[16:17, :] * (1.0 / D)
-    ratio = jnp.sum(jnp.sum(total[8:16] / cnew, axis=0, keepdims=True), axis=1, keepdims=True)
-    root = jnp.sqrt(jnp.broadcast_to(ratio, (1, 128)) * average * (1.0 / (float(D) * float(FF))))
+        ratio = ratio + sgat[i, 1:2]
+    ratio = jnp.broadcast_to(jnp.sum(ratio, axis=1, keepdims=True), (1, 128))
+    root = jnp.sqrt(ratio * average * (1.0 / (float(D) * float(FF))))
     scale = jnp.sqrt(average) / jnp.maximum(1.0, root)
-    rowfac = lax.rsqrt(rcol[...]) * scale
-    smine_free = lax.rsqrt(cnew)
-    spair[pl.ds(0, 8), :] = smine_free
-
-    def update_step(q, carry):
-        stepb[:, tile(q)] = (grad[:, tile(q)] * rowfac * spair[pl.ds(q, 1), :]).astype(BF)
+    colfac = []
+    for q in range(NZ):
+        col_out[pl.ds(q, 1), :] = sgat[q, 0:1]
+        colfac.append(jnp.broadcast_to(lax.rsqrt(sgat[q, 0:1]), (32, 128)))
+
+    def update_step(i, carry):
+        rows = pl.ds(pl.multiple_of(i * 32, 32), 32)
+        rowfac = lax.rsqrt(rcol[rows, :]) * scale
+        for q in range(8):
+            step_out[rows, tile(q)] = (grad[rows, tile(q)] * rowfac * colfac[q]).astype(BF)
         return carry
 
-    lax.fori_loop(0, 8, update_step, 0)
-    step_copy = pltpu.make_async_copy(stepb, step_out, o_s.at[2])
-    step_copy.start()
+    lax.fori_loop(0, ROWS // 32, update_step, 0)
 
     for copies in gathers:
         for copy in copies:
             copy.wait_send()
     weights.wait_send()
     for copies in inputs_copies:
-        for copy in copies:
+        for copy in copies.values():
             copy.wait_send()
     partial.wait_send()
-    pair.wait_send()
-    for copy in sums:
+    for copy in sums + shares:
         copy.wait_send()
 
     @pl.when(s > 0)
@@ -257,6 +343,8 @@
             for k in range(NZ):
                 lowered_copy(slot, k).wait_send()
 
+    pass_on(0, NZ, lambda slot, k: forward_copy(slot, k).wait_send())
+
     @pl.when(s < LAST)
     def _():
         for slot in range(2):
@@ -267,10 +355,6 @@
     def _():
         for i in range(NZ):
             pltpu.make_async_copy(zbuf, up_out.at[:, pl.ds(i * 2 * ROWS, 2 * ROWS)], z_s.at[i]).wait()
-
-    row_copy.wait()
-    col_copy.wait()
-    step_copy.wait()
 
 
 def place(*refs):
@@ -295,7 +379,7 @@
             jax.ShapeDtypeStruct((FF // 128, 128), F32),
         ),
         in_specs=[hbm] * 6,
-        out_specs=(hbm,) * 4,
+        out_specs=(hbm,) + (pl.BlockSpec(memory_space=pltpu.VMEM),) * 3,
         scratch_shapes=[
             pltpu.VMEM((TOK, FF), BF),
             pltpu.VMEM((TOK, FF), BF),
@@ -306,24 +390,25 @@
             pltpu.VMEM((ROWS, FF), F32),
             pltpu.VMEM((ROWS, FF), BF),
             pltpu.VMEM((ROWS, FF), BF),
-            pltpu.VMEM((ROWS, FF), BF),
             pltpu.VMEM((ROWS, 128), F32),
             pltpu.VMEM((ROWS // 128, 128), F32),
             pltpu.VMEM((FF // 128, 128), F32),
-            pltpu.VMEM((24, 128), F32),
-            pltpu.VMEM((24, 128), F32),
-            pltpu.VMEM((NZ, 24, 128), F32),
+            pltpu.VMEM((NZ, 4, 128), F32),
+            pltpu.VMEM((2, NZ, 4, 128), F32),
+            pltpu.VMEM((NZ, 2, 128), F32),
             pltpu.VMEM((TOK, 2 * ROWS), BF),
+            pltpu.VMEM((2, NZ, TOK, ROWS), BF),
             dma((7,)),
             dma((2, 4)), dma((2, 4)),
             dma(()), dma(()),
             dma((2, NZ)), dma((2, NZ)),
             dma((2, NZ)), dma((2, NZ)),
             dma(()), dma(()),
-            dma(()), dma(()),
             dma((NZ,)), dma((NZ,)),
-            dma((3,)),
+            dma((2, NZ)), dma((2, NZ)),
             dma((NZ,)),
+            dma((2, NZ)), dma((2, NZ)),
+            pltpu.SemaphoreType.REGULAR,
         ],
         compiler_params=pltpu.CompilerParams(collective_id=0, has_side_effects=True, vmem_limit_bytes=32 << 20),
         cost_estimate=pl.CostEstimate(flops=4 * 1024 * 1024 * 1024, transcendentals=TOK * FF, bytes_accessed=8 << 20),

time: 126 us -> 124 us (0.984)
  Pallas kernels: 125 us -> 122 us
    pallas_call x1, Pallas kernels: 123 us -> 121 us  [local(): pl.pallas_call(body, name='relay_step', out_shape=(jax.ShapeDtypeStruct((...]
where the time goes in v3:
time: 124 us; the launch traced here: 123 us
  Pallas kernels  122 us (98%)
    pallas_call x1, Pallas kernels, local(): pl.pallas_call(body, name='relay_step', out_shape=(jax.ShapeDtypeStruct((...  121 us

profile of v3, /device:TPU:2, one launch (start us, length us, event | category | flops | bytes accessed | tf_op | source)
XLA Modules:
  0.0 123.0 jit_solution(12847519579417156100)
XLA Ops:
  0.6 120.6 %relay_step.1 = (bf16[128,8192]{1,0:T(8,128)(2,1)S(1)}, bf16[512,1024]{1,0:T(8,128)(2,1)S(1)}, f32[4,128]{1,0:T(4,128)S(1)}, f32[8,128]{1,0:T(8,128)S(1)}) custom-call(bf16[128,8192]{1,0:T(8,128)(2,1)} %x_hbm.1, bf16[128,1024]{1,0:T(8,128)(2,1)} %hg_hbm.1, bf16[128,1024]{1,0:T(8,128)(2,1)} %gp_hbm.1, bf16[512,1024]{1,0:T(8,128)(2,1)} %w_hbm.1, ...), custom_call_target="tpu_custom_call" | custom-call | flops 4294967296 | bytes 8388608 | tf_op jit(solution)/shard_map/relay_step/pallas_call | solution.py:372
  121.3 1.7 %place_outputs.1 = (bf16[128,8192]{1,0:T(8,128)(2,1)}, bf16[512,1024]{1,0:T(8,128)(2,1)}, f32[4,128]{1,0:T(4,128)}, f32[8,128]{1,0:T(8,128)}) custom-call(bf16[128,8192]{1,0:T(8,128)(2,1)S(1)} %get-tuple-element.12.refs_0_, bf16[512,1024]{1,0:T(8,128)(2,1)S(1)} %get-tuple-element.13.refs_1_, f32[4,128]{1,0:T(4,128)S(1)} %get-tuple-element.14.refs_2_, ...), custom_call_target="tpu_custom_call" | custom-call | tf_op jit(solution)/shard_map/place_outputs/pallas_call | solution.py:422

commit v4 on v3

--- a/solution.py
+++ b/solution.py
@@ -301,8 +301,8 @@
     shares = [remote(sgat.at[z], sgat.at[z], p_s.at[k], p_r.at[k], device(s, xh, ring(k))) for k in FAR_FIRST]
     for copy in shares:
         copy.start()
+    lowered_send(ORDER[10:14])
     pass_on(4, NZ, pass_start)
-    lowered_send(ORDER[10:14])
     average = total[2:3] * (1.0 / D)
     for copy in shares:
         copy.wait_recv()

time: 124 us -> 124 us (level)
  no operation moved by 1% of the time
where the time goes in v4:
time: 124 us; the launch traced here: 123 us
  Pallas kernels  122 us (98%)
    pallas_call x1, Pallas kernels, local(): pl.pallas_call(body, name='relay_step', out_shape=(jax.ShapeDtypeStruct((...  121 us

profile of v4, /device:TPU:2, one launch (start us, length us, event | category | flops | bytes accessed | tf_op | source)
XLA Modules:
  0.0 123.0 jit_solution(9401639491316751747)
XLA Ops:
  0.6 120.6 %relay_step.1 = (bf16[128,8192]{1,0:T(8,128)(2,1)S(1)}, bf16[512,1024]{1,0:T(8,128)(2,1)S(1)}, f32[4,128]{1,0:T(4,128)S(1)}, f32[8,128]{1,0:T(8,128)S(1)}) custom-call(bf16[128,8192]{1,0:T(8,128)(2,1)} %x_hbm.1, bf16[128,1024]{1,0:T(8,128)(2,1)} %hg_hbm.1, bf16[128,1024]{1,0:T(8,128)(2,1)} %gp_hbm.1, bf16[512,1024]{1,0:T(8,128)(2,1)} %w_hbm.1, ...), custom_call_target="tpu_custom_call" | custom-call | flops 4294967296 | bytes 8388608 | tf_op jit(solution)/shard_map/relay_step/pallas_call | solution.py:372
  121.3 1.7 %place_outputs.1 = (bf16[128,8192]{1,0:T(8,128)(2,1)}, bf16[512,1024]{1,0:T(8,128)(2,1)}, f32[4,128]{1,0:T(4,128)}, f32[8,128]{1,0:T(8,128)}) custom-call(bf16[128,8192]{1,0:T(8,128)(2,1)S(1)} %get-tuple-element.12.refs_0_, bf16[512,1024]{1,0:T(8,128)(2,1)S(1)} %get-tuple-element.13.refs_1_, f32[4,128]{1,0:T(4,128)S(1)} %get-tuple-element.14.refs_2_, ...), custom_call_target="tpu_custom_call" | custom-call | tf_op jit(solution)/shard_map/place_outputs/pallas_call | solution.py:422
